TPU v7x, 32 devices: a whole 2x2x4 slice. The times are simulated.
32 devices in a mesh: macro: 16 (over z, x, core), vox: 2 (over y).
Axes of the slice: x: 2, y: 2, z: 4, core: 2. Of those that a mesh axis runs over, the one named last changes fastest.
Arguments:
- displacement: float32 [3, 1024], P(None, 'macro'), may hold values from -1.2 to 1.2
- load: float32 [3, 1024], P(None, 'macro'), may hold values from -6 to 6
- conn: int32 [8, 1024], P(None, 'macro'), may hold values from 0 to 79
- halo_list: int32 [256], P('macro'), may hold values from 0 to 63
- grad_ops: float32 [3, 8, 1024], P(None, None, 'macro'), may hold values from -3 to 3
- volume: float32 [1024], P('macro'), may hold values from 0.5 to 2
- elastic_moduli: float32 [2, 1024], P(None, 'macro'), may hold values from 1 to 4
- plastic_mask: int32 [1024], P('macro'), may hold values from 0 to 1, as said below
- new_owner: int32 [1024], P('macro'), may hold values from -1 to 15, as said below
- state: float32 [7, 1024, 16, 256], P(None, 'macro', 'vox'), may hold values from -0.6 to 1, as said below
- micro_moduli: float32 [4, 16, 256], P(None, 'vox'), may hold values from 0.5 to 6
Outputs:
- residual: float32 [3, 1024], P(None, 'macro')
- moved_state: float32 [7, 384, 16, 256], P(None, 'macro', 'vox')
Inputs may be any that keep to these rules, and one draw needn't show every extreme that they name: `plastic_mask`: each group's 64 points hold at most 48 plastic ones, 384 in all. `new_owner`: -1 exactly at elastic points; every group becomes the owner of exactly 24 plastic points, at most 3 of them from any one group. `state`: component 6 is nonnegative.
All inputs are finite; a program needn't handle non-finite values.
Results may differ from a plain program's by a relative error of at most 0.0001.
Values sent between devices are 32-bit elements; how exact they have to be, the bound alone decides.
A program may use at most 64 MiB of HBM per device.

v0:
```python
import math
import jax
import jax.numpy as jnp
from jax import lax
from jax.sharding import PartitionSpec as P

RECV_AGG = 24
PLASTIC_MAX = 48
VOX_SIDE = 16
VOX_PLANE = 256
SWEEPS = 4
LAM_REF = 3.0
MU_REF = 3.0
FULL_PREC = lax.Precision.HIGHEST


def shifted(block, axis, distance):
    devices = range(lax.axis_size(axis))
    route = [((i - distance) % len(devices), i) for i in devices]
    return lax.ppermute(block, axis, route)


def strain_tensor(disp_el, grad_el):
    products = [[jnp.sum(disp_el[i] * grad_el[j], axis=0) for j in range(3)] for i in range(3)]
    return jnp.stack(
        [
            products[0][0],
            products[1][1],
            products[2][2],
            0.5 * (products[1][2] + products[2][1]),
            0.5 * (products[0][2] + products[2][0]),
            0.5 * (products[0][1] + products[1][0]),
        ]
    )


def full_tensor(voigt):
    return [
        [voigt[0], voigt[5], voigt[4]],
        [voigt[5], voigt[1], voigt[3]],
        [voigt[4], voigt[3], voigt[2]],
    ]


def nodal_forces(stress, grad_el, volume):
    tensor = full_tensor(stress)
    return jnp.stack(
        [
            volume
            * (tensor[i][0] * grad_el[0] + tensor[i][1] * grad_el[1] + tensor[i][2] * grad_el[2])
            for i in range(3)
        ]
    )


def elastic_stress(strain, moduli):
    lame_first = moduli[0]
    shear_mod = moduli[1]
    trace = strain[0] + strain[1] + strain[2]
    return jnp.stack(
        [lame_first * trace + 2.0 * shear_mod * strain[c] for c in range(3)]
        + [2.0 * shear_mod * strain[c] for c in range(3, 6)]
    )


def return_map(strain, state, props):
    lame_first, shear_mod, yield_base, harden = (props[0], props[1], props[2], props[3])
    elastic = [strain[c] - state[c] for c in range(6)]
    trace = elastic[0] + elastic[1] + elastic[2]
    trial = [lame_first * trace + 2.0 * shear_mod * elastic[c] for c in range(3)] + [
        2.0 * shear_mod * elastic[c] for c in range(3, 6)
    ]
    pressure = (trial[0] + trial[1] + trial[2]) / 3.0
    deviator = [
        trial[0] - pressure,
        trial[1] - pressure,
        trial[2] - pressure,
        trial[3],
        trial[4],
        trial[5],
    ]
    squared = (
        deviator[0] ** 2
        + deviator[1] ** 2
        + deviator[2] ** 2
        + 2.0 * (deviator[3] ** 2 + deviator[4] ** 2 + deviator[5] ** 2)
    )
    equivalent = jnp.sqrt(1.5 * squared)
    strength = yield_base + harden * state[6]
    excess = jnp.maximum(equivalent - strength, 0.0)
    stiffer = 3.0 * shear_mod + harden
    factor = excess / (stiffer * jnp.maximum(equivalent, strength))
    stress = jnp.stack([trial[c] - 3.0 * shear_mod * factor * deviator[c] for c in range(6)])
    new_state = jnp.stack(
        [state[c] + 1.5 * factor * deviator[c] for c in range(6)] + [state[6] + excess / stiffer]
    )
    return (stress, new_state)


def green_apply(tau, freq_x, freq_y, freq_z):
    trac_x = tau[0] * freq_x + tau[5] * freq_y + tau[4] * freq_z
    trac_y = tau[5] * freq_x + tau[1] * freq_y + tau[3] * freq_z
    trac_z = tau[4] * freq_x + tau[3] * freq_y + tau[2] * freq_z
    norm_sq = freq_x * freq_x + freq_y * freq_y + freq_z * freq_z
    inverse = jnp.where(norm_sq > 0, 1.0 / jnp.maximum(norm_sq, 1.0), 0.0)
    coupling = (LAM_REF + MU_REF) / (LAM_REF + 2.0 * MU_REF)
    along = (freq_x * trac_x + freq_y * trac_y + freq_z * trac_z) * inverse
    wave_x = (trac_x - coupling * along * freq_x) * inverse / MU_REF
    wave_y = (trac_y - coupling * along * freq_y) * inverse / MU_REF
    wave_z = (trac_z - coupling * along * freq_z) * inverse / MU_REF
    return [
        freq_x * wave_x,
        freq_y * wave_y,
        freq_z * wave_z,
        0.5 * (freq_y * wave_z + freq_z * wave_y),
        0.5 * (freq_x * wave_z + freq_z * wave_x),
        0.5 * (freq_x * wave_y + freq_y * wave_x),
    ]


def dft_tables():
    line_index = jnp.arange(VOX_SIDE, dtype=jnp.int32)
    line_phase = line_index[:, None] * line_index[None, :] % VOX_SIDE
    plane_index = jnp.arange(VOX_PLANE, dtype=jnp.int32)
    plane_rows = plane_index // VOX_SIDE
    plane_cols = plane_index % VOX_SIDE
    plane_phase = (
        plane_rows[:, None] * plane_rows[None, :] + plane_cols[:, None] * plane_cols[None, :]
    ) % VOX_SIDE
    radians = 2.0 * math.pi / VOX_SIDE
    line_angle = line_phase.astype(jnp.float32) * radians
    plane_angle = plane_phase.astype(jnp.float32) * radians
    signed = jnp.where(line_index < VOX_SIDE // 2, line_index, line_index - VOX_SIDE).astype(
        jnp.float32
    )
    return (
        jnp.cos(line_angle),
        jnp.sin(line_angle),
        jnp.cos(plane_angle),
        jnp.sin(plane_angle),
        signed[:, None],
        signed[plane_rows],
        signed[plane_cols],
    )


def line_apply(table, field):
    return jnp.einsum("kx,cbxn->cbkn", table, field, precision=FULL_PREC)


def spectral_correction(stress, tables):
    cos_line, sin_line, cos_plane, sin_plane, freq_x, freq_y, freq_z = tables
    real_plane = jnp.dot(stress, cos_plane, precision=FULL_PREC)
    imag_plane = -jnp.dot(stress, sin_plane, precision=FULL_PREC)
    real_full = line_apply(cos_line, real_plane) + line_apply(sin_line, imag_plane)
    imag_full = line_apply(cos_line, imag_plane) - line_apply(sin_line, real_plane)
    green_real = jnp.stack(green_apply([real_full[c] for c in range(6)], freq_x, freq_y, freq_z))
    green_imag = jnp.stack(green_apply([imag_full[c] for c in range(6)], freq_x, freq_y, freq_z))
    back_real = line_apply(cos_line, green_real) - line_apply(sin_line, green_imag)
    back_imag = line_apply(cos_line, green_imag) + line_apply(sin_line, green_real)
    spatial = jnp.dot(back_real, cos_plane, precision=FULL_PREC) - jnp.dot(
        back_imag, sin_plane, precision=FULL_PREC
    )
    return spatial / VOX_SIDE**3


def micro_solve(states, strains, moduli_slab):
    tables = dft_tables()
    aggregates = states.shape[1]
    thickness = states.shape[2]
    ranks_vox = lax.axis_size("vox")
    per_rank = aggregates // ranks_vox
    full_moduli = lax.all_gather(moduli_slab, "vox", axis=1, tiled=True)
    gathered = lax.all_to_all(
        states.reshape(7, ranks_vox, per_rank, thickness, VOX_PLANE),
        "vox",
        split_axis=1,
        concat_axis=3,
        tiled=True,
    )
    gathered = gathered.reshape(7, per_rank, VOX_SIDE, VOX_PLANE)
    own_strain = lax.dynamic_slice_in_dim(strains, lax.axis_index("vox") * per_rank, per_rank, 1)
    strain_field = jnp.broadcast_to(own_strain[:, :, None, None], (6,) + gathered.shape[1:])
    for iteration in range(SWEEPS):
        stress, _ = return_map(strain_field, gathered, full_moduli)
        strain_field = strain_field - spectral_correction(stress, tables)
    stress, updated = return_map(strain_field, gathered, full_moduli)
    averaged = lax.all_gather(jnp.mean(stress, axis=(2, 3)), "vox", axis=1, tiled=True)
    returned = lax.all_to_all(
        updated.reshape(7, per_rank, ranks_vox, thickness, VOX_PLANE),
        "vox",
        split_axis=2,
        concat_axis=1,
        tiled=True,
    )
    return (returned.reshape(states.shape), averaged)


def pick_slots(valid, count):
    position = jnp.cumsum(valid.astype(jnp.int32)) - 1
    wanted = jnp.arange(count, dtype=jnp.int32)
    matching = (wanted[:, None] == position[None, :]) & valid[None, :]
    sources = jnp.arange(valid.shape[0], dtype=jnp.int32)
    return (jnp.sum(jnp.where(matching, sources[None, :], 0), axis=1), matching)


def local(
    displacement,
    load,
    conn,
    halo_list,
    grad_ops,
    volume,
    elastic_moduli,
    plastic_mask,
    new_owner,
    state,
    micro_moduli,
):
    groups = lax.axis_size("macro")
    own_nodes = displacement.shape[1]
    elements = conn.shape[1]
    halo_disp = shifted(displacement[:, halo_list], "macro", 1)
    local_disp = jnp.concatenate([displacement, halo_disp], axis=1)
    strain = strain_tensor(local_disp[:, conn], grad_ops)
    plastic = plastic_mask == 1
    point_ids = jnp.arange(elements, dtype=jnp.int32)
    same_owner = (
        (new_owner[:, None] == new_owner[None, :])
        & plastic[:, None]
        & plastic[None, :]
        & (point_ids[None, :] < point_ids[:, None])
    )
    owner_rank = jnp.sum(same_owner.astype(jnp.int32), axis=1)
    capacity = (PLASTIC_MAX + groups - 1) // groups
    send_slot = jnp.where(plastic, new_owner * capacity + owner_rank, -1)
    slot_ids = jnp.arange(groups * capacity, dtype=jnp.int32)
    slot_match = slot_ids[:, None] == send_slot[None, :]
    slot_valid = jnp.any(slot_match, axis=1)
    valid_float = slot_valid.astype(jnp.float32)
    slot_source = jnp.sum(jnp.where(slot_match, point_ids[None, :], 0), axis=1)
    outgoing = state[:, slot_source] * valid_float[None, :, None, None]
    strain_rows = strain[:, slot_source] * valid_float[None, :]
    received, got_strain, got_valid = (
        lax.all_to_all(outgoing, "macro", split_axis=1, concat_axis=1, tiled=True),
        lax.all_to_all(strain_rows, "macro", split_axis=1, concat_axis=1, tiled=True),
        lax.all_to_all(valid_float[None, :], "macro", split_axis=1, concat_axis=1, tiled=True),
    )
    recv_index, recv_match = pick_slots(got_valid[0] > 0.5, RECV_AGG)
    moved_state, averaged = micro_solve(
        received[:, recv_index], got_strain[:, recv_index], micro_moduli
    )
    slot_stress = jnp.dot(averaged, recv_match.astype(jnp.float32), precision=FULL_PREC)
    got_stress = lax.all_to_all(slot_stress, "macro", split_axis=1, concat_axis=1, tiled=True)
    stress_plastic = jnp.dot(got_stress, slot_match.astype(jnp.float32), precision=FULL_PREC)
    stress = jnp.where(plastic[None, :], stress_plastic, elastic_stress(strain, elastic_moduli))
    forces = nodal_forces(stress, grad_ops, volume)
    node_ids = jnp.arange(local_disp.shape[1], dtype=jnp.int32)
    node_match = (conn[:, :, None] == node_ids[None, None, :]).astype(jnp.float32)
    assembled = jnp.einsum("iae,aen->in", forces, node_match, precision=FULL_PREC)
    returned_force = shifted(assembled[:, own_nodes:], "macro", -1)
    own_ids = jnp.arange(own_nodes, dtype=jnp.int32)
    halo_match = (halo_list[:, None] == own_ids[None, :]).astype(jnp.float32)
    residual = (
        assembled[:, :own_nodes] + jnp.dot(returned_force, halo_match, precision=FULL_PREC) - load
    )
    return (residual, moved_state)


def solution(mesh):
    return jax.shard_map(
        local,
        mesh=mesh,
        in_specs=(
            P(None, "macro"),
            P(None, "macro"),
            P(None, "macro"),
            P("macro"),
            P(None, None, "macro"),
            P("macro"),
            P(None, "macro"),
            P("macro"),
            P("macro"),
            P(None, "macro", "vox", None),
            P(None, "vox", None),
        ),
        out_specs=(P(None, "macro"), P(None, "macro", "vox", None)),
        check_vma=False,
    )
```

profile of v0, /device:TPU:0, one launch (start us, length us, event | category | flops | bytes accessed | tf_op | source)
XLA Modules:
  0.0 243.6 jit_solution(13568793401414966940)
XLA Ops:
  3.7 7.4 %all-to-all-start.1 = ((f32[1,16,3]{2,0,1:T(1,128)}), f32[1,16,3]{2,0,1:T(1,128)S(1)}, u32[]{:S(2)}, u32[]{:S(2)}) async-start(f32[1,16,3]{2,0,1:T(1,128)} %bitcast.13), calls=%async_computation.1 | async-start | bytes 16384 | tf_op jit(solution)/shard_map/all_to_all | solution.py:247
  11.9 2.8 %gather_fusion.4 = f32[48,7,8,256]{3,2,1,0:T(8,128)S(1)} fusion(f32[7,64,8,256]{3,2,1,0:T(8,128)} %param.20, s32[1024]{0:T(1024)S(1)} %get-tuple-element.240), kind=kCustom, calls=%fused_computation.4 | custom fusion | bytes 5505216 | tf_op jit(solution)/shard_map/gather | solution.py:242
  14.7 1.8 multiply_bitcast_fusion
  17.5 5.2 %all-to-all-start.2 = ((f32[7,48,8,256]{3,2,0,1:T(8,128)}), f32[7,48,8,256]{3,2,0,1:T(8,128)S(1)}, u32[]{:S(2)}, u32[]{:S(2)}) async-start(f32[7,48,8,256]{3,2,0,1:T(8,128)} %multiply_bitcast_fusion), calls=%async_computation.2 | async-start | bytes 5505024 | tf_op jit(solution)/shard_map/all_to_all | solution.py:245
  25.3 4.2 %compare_select_fusion.3 = (f32[256,1]{0,1:T(1,128)S(1)}, f32[256,1]{0,1:T(1,128)S(1)}) fusion(f32[]{:T(128)} %bitcast.53, f32[]{:T(128)} %bitcast.54, f32[]{:T(128)} %bitcast.55, f32[]{:T(128)} %bitcast.56, f32[]{:T(128)} %bitcast.57, f32[]{:T(128)} %bitcast.59, f32[]{:T(128)} %bitcast.58), kind=kLoop, calls=%fused_computation.506 | loop fusion | flops 10752 | bytes 2076 | tf_op jit(solution)/shard_map/gather | solution.py:143
  29.5 5.6 %broadcast_multiply_fusion.1 = (f32[256]{0:T(256)S(1)}, f32[256]{0:T(256)S(1)}) fusion(pred[256]{0:T(512)(128)(4,1)S(1)} %compare_reduce_fusion.1, pred[256]{0:T(512)(128)(4,1)S(1)} %compare_reduce_fusion.2, pred[256]{0:T(512)(128)(4,1)S(1)} %compare_reduce_fusion.3, pred[256]{0:T(512)(128)(4,1)S(1)} %compare_reduce_fusion.4, ...), kind=kLoop, calls=%fused_computation.559 | loop fusion | flops 2560 | bytes 5412 | tf_op jit(solution)/shard_map/mul | solution.py:114
  35.2 5.6 %broadcast_multiply_fusion.2 = (f32[256]{0:T(256)S(1)}, f32[256]{0:T(256)S(1)}) fusion(pred[256]{0:T(512)(128)(4,1)S(1)} %compare_reduce_fusion.10, pred[256]{0:T(512)(128)(4,1)S(1)} %compare_reduce_fusion.11, pred[256]{0:T(512)(128)(4,1)S(1)} %compare_reduce_fusion.12, pred[256]{0:T(512)(128)(4,1)S(1)} %compare_reduce_fusion.13, ...), kind=kLoop, calls=%fused_computation.560 | loop fusion | flops 2560 | bytes 5412 | tf_op jit(solution)/shard_map/mul | solution.py:113
  40.9 31.7 %collective-permute-done = f32[3,16]{0,1:T(8,128)S(1)} collective-permute-done((f32[3,16]{0,1:T(8,128)S(1)}, f32[3,16]{0,1:T(8,128)S(1)}, u32[]{:S(2)}, u32[]{:S(2)}) %collective-permute-start) | collective-permute-done | bytes 224 | tf_op jit(solution)/shard_map/ppermute | solution.py:20
  76.2 15.5 %all-to-all-start = ((f32[6,16,3]{0,2,1:T(4,128)}), f32[6,16,3]{0,2,1:T(4,128)S(1)}, u32[]{:S(2)}, u32[]{:S(2)}) async-start(f32[6,16,3]{0,2,1:T(4,128)} %copy.230), calls=%async_computation | async-start | bytes 65536 | tf_op jit(solution)/shard_map/all_to_all | solution.py:246
  91.7 1.8 copy.236
  93.5 2.4 gather_fusion.5
  95.9 1.2 copy.238
  98.3 3.6 %all-to-all-start.3 = ((f32[7,2,12,8,256]{4,3,2,0,1:T(8,128)}), f32[7,2,12,8,256]{4,3,2,0,1:T(8,128)S(1)}, u32[]{:S(2)}, u32[]{:S(2)}) async-start(f32[7,2,12,8,256]{4,3,2,0,1:T(8,128)} %copy.238), calls=%async_computation.3 | async-start | bytes 2752512 | tf_op jit(solution)/shard_map/all_to_all | solution.py:174
  102.0 17.9 %all_gather.6 = f32[4,16,256]{2,1,0:T(8,128)S(1)} all-gather(f32[4,8,256]{2,1,0:T(8,128)S(1)} %copy-done.1), channel_id=1, replica_groups=mesh['macro'=16,'vox'=2] {'vox'}, dimensions={1}, use_global_device_ids=true | all-gather | bytes 98304 | tf_op jit(solution)/shard_map/all_gather | solution.py:173
  121.9 2.1 fusion.42
  124.1 2.1 convolution_negate_fusion.3
  126.2 1.2 fusion.204
  128.6 1.2 fusion.23
  129.8 1.2 fusion.22
  132.2 1.4 fusion.198
  135.9 1.2 fusion.21
  137.1 2.1 fusion.40
  139.2 2.2 fusion.7
  142.1 2.1 fusion.38
  144.3 2.5 %convolution_negate_fusion.2 = f32[6,12,16,256]{3,2,1,0:T(8,128)S(1)} fusion(f32[6,12,16,256]{3,2,1,0:T(8,128)S(1)} %fusion.57, s32[256]{0:T(256)S(1)} %get-tuple-element.244, s32[256]{0:T(256)S(1)} %get-tuple-element.245), kind=kOutput, calls=%fused_computation.18 | convolution fusion | flops 907313152 | bytes 2361344 | tf_op jit(solution)/shard_map/dot_general | solution.py:154
  149.2 1.2 fusion.19
  157.4 2.3 fusion.36
  159.8 2.2 fusion.5
  162.6 2.1 fusion.34
  164.8 2.1 convolution_negate_fusion.1
  169.3 1.4 fusion.15
  175.4 1.2 fusion.12
  177.8 2.1 fusion.32
  179.9 2.6 %fusion.3 = f32[6,12,16,256]{3,2,1,0:T(8,128)S(1)} fusion(f32[6,12,16,256]{3,2,1,0:T(8,128)S(1)} %fusion.5, f32[6,12,16,256]{3,2,1,0:T(8,128)S(1)} %fusion.32, f32[6,12,16,256]{3,2,1,0:T(8,128)S(1)} %fusion.12, s32[256]{0:T(256)S(1)} %get-tuple-element.244, s32[256]{0:T(256)S(1)} %get-tuple-element.245), kind=kOutput, calls=%fused_computation.13 | convolution fusion | flops 907902976 | bytes 4720640 | tf_op jit(solution)/shard_map/dot_general | solution.py:161
  183.2 2.1 fusion.30
  185.3 2.1 convolution_negate_fusion
  193.4 1.4 fusion.174
  197.1 1.2 fusion.9
  198.3 2.2 fusion.28
  200.5 2.2 fusion.1
  203.8 4.4 %all-gather = f32[2,12,6]{1,2,0:T(8,128)S(1)} all-gather(f32[1,12,6]{1,2,0:T(8,128)S(1)} %multiply_bitcast_fusion.2), channel_id=1, replica_groups=mesh['macro'=16,'vox'=2] {'vox'}, dimensions={0}, use_global_device_ids=true | all-gather | bytes 864 | tf_op jit(solution)/shard_map/all_gather | solution.py:188
  209.3 5.4 %all-to-all-start.4 = ((f32[6,16,3]{0,2,1:T(4,128)}), f32[6,16,3]{0,2,1:T(4,128)S(1)}, u32[]{:S(2)}, u32[]{:S(2)}) async-start(f32[6,16,3]{0,2,1:T(4,128)} %copy.247), calls=%async_computation.4 | async-start | bytes 65536 | tf_op jit(solution)/shard_map/all_to_all | solution.py:254
  214.8 1.2 copy.267
  216.0 5.3 %all-to-all-done.4 = f32[6,16,3]{0,2,1:T(4,128)S(1)} async-done(((f32[6,16,3]{0,2,1:T(4,128)}), f32[6,16,3]{0,2,1:T(4,128)S(1)}, u32[]{:S(2)}, u32[]{:S(2)}) %all-to-all-start.4) | async-done | bytes 1184 | tf_op jit(solution)/shard_map/all_to_all | solution.py:254
  221.4 3.6 %all-to-all-start.5 = ((f32[7,12,2,8,256]{4,3,1,0,2:T(8,128)}), f32[7,12,2,8,256]{4,3,1,0,2:T(8,128)S(1)}, u32[]{:S(2)}, u32[]{:S(2)}) async-start(f32[7,12,2,8,256]{4,3,1,0,2:T(8,128)} %copy.267), calls=%async_computation.5 | async-start | bytes 2752512 | tf_op jit(solution)/shard_map/all_to_all | solution.py:189
  225.8 1.3 collective-permute-done.1
  227.9 14.3 %all-to-all-done.5 = f32[7,12,2,8,256]{4,3,1,0,2:T(8,128)S(1)} async-done(((f32[7,12,2,8,256]{4,3,1,0,2:T(8,128)}), f32[7,12,2,8,256]{4,3,1,0,2:T(8,128)S(1)}, u32[]{:S(2)}, u32[]{:S(2)}) %all-to-all-start.5) | async-done | bytes 1376288 | tf_op jit(solution)/shard_map/all_to_all | solution.py:189
  242.2 1.2 copy.257
  (192 shorter events, 50.3 us)
Async XLA Ops:
  3.7 13.8 %all-to-all-start.1 = ((f32[1,16,3]{2,0,1:T(1,128)}), f32[1,16,3]{2,0,1:T(1,128)S(1)}, u32[]{:S(2)}, u32[]{:S(2)}) async-start(f32[1,16,3]{2,0,1:T(1,128)} %bitcast.13), calls=%async_computation.1 | async-start | bytes 16384 | tf_op jit(solution)/shard_map/all_to_all | solution.py:247
  16.5 6.2 %copy-start.4 = (f32[3,64]{1,0:T(4,128)S(1)}, f32[3,64]{1,0:T(4,128)}, u32[]{:S(2)}) copy-start(f32[3,64]{1,0:T(4,128)} %param.11) | copy-start | bytes 2308
  16.5 7.4 %copy-start.2 = (s32[8,64]{1,0:T(8,128)S(1)}, s32[8,64]{1,0:T(8,128)}, u32[]{:S(2)}) copy-start(s32[8,64]{1,0:T(8,128)} %param.13) | copy-start | bytes 6148
  16.5 57.3 %copy-start = (f32[3,8,64]{2,1,0:T(8,128)S(1)}, f32[3,8,64]{2,1,0:T(8,128)}, u32[]{:S(2)}) copy-start(f32[3,8,64]{2,1,0:T(8,128)} %param.15) | copy-start | bytes 18436
  16.5 57.4 %copy-start.3 = (f32[2,64]{1,0:T(2,128)S(1)}, f32[2,64]{1,0:T(2,128)}, u32[]{:S(2)}) copy-start(f32[2,64]{1,0:T(2,128)} %param.17) | copy-start | bytes 1540
  17.5 58.7 %all-to-all-start.2 = ((f32[7,48,8,256]{3,2,0,1:T(8,128)}), f32[7,48,8,256]{3,2,0,1:T(8,128)S(1)}, u32[]{:S(2)}, u32[]{:S(2)}) async-start(f32[7,48,8,256]{3,2,0,1:T(8,128)} %multiply_bitcast_fusion), calls=%async_computation.2 | async-start | bytes 5505024 | tf_op jit(solution)/shard_map/all_to_all | solution.py:245
  23.3 49.3 %collective-permute-start = (f32[3,16]{0,1:T(8,128)S(1)}, f32[3,16]{0,1:T(8,128)S(1)}, u32[]{:S(2)}, u32[]{:S(2)}) collective-permute-start(f32[3,16]{0,1:T(8,128)S(1)} %bitcast.583), channel_id=1, source_target_pairs={{30,0},{0,2},{2,4},{4,6},{6,8},{8,10},{10,12},{12,14},{14,16},{16,... | collective-permute-start | bytes 584 | tf_op jit(solution)/shard_map/ppermute | solution.py:20
  76.2 22.1 %all-to-all-start = ((f32[6,16,3]{0,2,1:T(4,128)}), f32[6,16,3]{0,2,1:T(4,128)S(1)}, u32[]{:S(2)}, u32[]{:S(2)}) async-start(f32[6,16,3]{0,2,1:T(4,128)} %copy.230), calls=%async_computation | async-start | bytes 65536 | tf_op jit(solution)/shard_map/all_to_all | solution.py:246
  97.1 4.8 %copy-start.1 = (f32[4,8,256]{2,1,0:T(8,128)S(1)}, f32[4,8,256]{2,1,0:T(8,128)}, u32[]{:S(2)}) copy-start(f32[4,8,256]{2,1,0:T(8,128)} %param.21) | copy-start | bytes 98308
  98.3 22.6 %all-to-all-start.3 = ((f32[7,2,12,8,256]{4,3,2,0,1:T(8,128)}), f32[7,2,12,8,256]{4,3,2,0,1:T(8,128)S(1)}, u32[]{:S(2)}, u32[]{:S(2)}) async-start(f32[7,2,12,8,256]{4,3,2,0,1:T(8,128)} %copy.238), calls=%async_computation.3 | async-start | bytes 2752512 | tf_op jit(solution)/shard_map/all_to_all | solution.py:174
  209.3 12.0 %all-to-all-start.4 = ((f32[6,16,3]{0,2,1:T(4,128)}), f32[6,16,3]{0,2,1:T(4,128)S(1)}, u32[]{:S(2)}, u32[]{:S(2)}) async-start(f32[6,16,3]{0,2,1:T(4,128)} %copy.247), calls=%async_computation.4 | async-start | bytes 65536 | tf_op jit(solution)/shard_map/all_to_all | solution.py:254
  216.0 9.2 %copy-start.5 = (f32[64]{0:T(128)S(1)}, f32[64]{0:T(128)}, u32[]{:S(2)}) copy-start(f32[64]{0:T(128)} %param.16) | copy-start | bytes 772
  216.0 11.1 %copy-start.6 = (f32[3,64]{1,0:T(4,128)S(1)}, f32[3,64]{1,0:T(4,128)}, u32[]{:S(2)}) copy-start(f32[3,64]{1,0:T(4,128)} %param.12) | copy-start | bytes 2308
  216.0 11.1 %copy-start.7 = (s32[16]{0:T(128)S(1)}, s32[16]{0:T(128)}, u32[]{:S(2)}) copy-start(s32[16]{0:T(128)} %param.14) | copy-start | bytes 196
  221.4 20.9 %all-to-all-start.5 = ((f32[7,12,2,8,256]{4,3,1,0,2:T(8,128)}), f32[7,12,2,8,256]{4,3,1,0,2:T(8,128)S(1)}, u32[]{:S(2)}, u32[]{:S(2)}) async-start(f32[7,12,2,8,256]{4,3,1,0,2:T(8,128)} %copy.267), calls=%async_computation.5 | async-start | bytes 2752512 | tf_op jit(solution)/shard_map/all_to_all | solution.py:189
  225.6 1.5 collective-permute-start.1
where the time goes:
time: 248 us; the launch traced here: 244 us
  matrix products  74.8 us (30%)
  waiting for transfers between devices  54.8 us (22%)
  starting transfers between devices  41.4 us (17%)
  other arithmetic  30.3 us (12%)
  blocking collectives  22.3 us (9%)
  local copies, waits for them, and re-layouts  18.1 us (7%)
    dot_general x32, matrix products, line_apply(): return jnp.einsum('kx,cbxn->cbkn', table, field, precision=FULL_PREC)  38.1 us
    ppermute x2, waiting for transfers between devices, shifted(): return lax.ppermute(block, axis, route)  33 us
    all_gather x1, blocking collectives, micro_solve(): full_moduli = lax.all_gather(moduli_slab, 'vox', axis=1, tiled=True)  17.9 us
    all_to_all x1, starting transfers between devices, local(): lax.all_to_all(strain_rows, 'macro', split_axis=1, concat_axis=1, tiled=T...  15.5 us
    all_to_all x1, waiting for transfers between devices, micro_solve(): lax.all_to_all(updated.reshape(7, per_rank, ranks_vox, thickness, VOX_PLA...  14.3 us
    dot_general x4, matrix products, spectral_correction(): jnp.dot(back_imag, sin_plane, precision=FULL_PREC)  9.12 us
    dot_general x4, matrix products, spectral_correction(): imag_plane = -jnp.dot(stress, sin_plane, precision=FULL_PREC)  8.95 us
    dot_general x4, matrix products, spectral_correction(): jnp.dot(back_real, cos_plane, precision=FULL_PREC)  8.75 us
  transfers between devices with their start and end apart: 8, of which 6 were waited for; matrix products, arithmetic and copies ran while one was open for 15% of the time, Pallas kernels for 0%

commit v1 on v0

--- a/solution.py
+++ b/solution.py
@@ -243,7 +243,12 @@
     strain_rows = strain[:, slot_source] * valid_float[None, :]
     received, got_strain, got_valid = (
         lax.all_to_all(outgoing, "macro", split_axis=1, concat_axis=1, tiled=True),
-        lax.all_to_all(strain_rows, "macro", split_axis=1, concat_axis=1, tiled=True),
+        jnp.concatenate(
+            lax.all_to_all(
+                jnp.stack(jnp.split(strain_rows, lax.axis_size("macro"), axis=1)), "macro", 0, 0
+            ),
+            axis=1,
+        ),
         lax.all_to_all(valid_float[None, :], "macro", split_axis=1, concat_axis=1, tiled=True),
     )
     recv_index, recv_match = pick_slots(got_valid[0] > 0.5, RECV_AGG)

time: 248 us -> 264 us (1.065)
  local copies, waits for them, and re-layouts: 18.1 us -> 27.1 us
  waiting for transfers between devices: 54.8 us -> 62.4 us
    all_to_all x1, waiting for transfers between devices: 0.01 us -> 40.3 us  [local(): lax.all_to_all(outgoing, 'macro', split_axis=1, concat_axis=1, tiled=True)]
    ppermute x2, waiting for transfers between devices: 33 us -> 1.31 us  [shifted(): return lax.ppermute(block, axis, route)]
    unnamed x18 -> x31, local copies, waits for them, and re-layouts: 0.21 us -> 9.7 us
  transfers between devices with their start and end apart: 8 -> 8, of which waited for: 6 -> 5; matrix products, arithmetic and copies ran while one was open for 15% -> 17% of each run, Pallas kernels for 0% -> 0%
where the time goes in v1:
time: 264 us; the launch traced here: 260 us
  matrix products  74.8 us (28%)
  waiting for transfers between devices  62.4 us (24%)
  starting transfers between devices  40.5 us (15%)
  other arithmetic  30.7 us (12%)
  local copies, waits for them, and re-layouts  27.1 us (10%)
  blocking collectives  22.3 us (8%)
    all_to_all x1, waiting for transfers between devices, local(): lax.all_to_all(outgoing, 'macro', split_axis=1, concat_axis=1, tiled=True)  40.3 us
    dot_general x32, matrix products, line_apply(): return jnp.einsum('kx,cbxn->cbkn', table, field, precision=FULL_PREC)  38 us
    all_gather x1, blocking collectives, micro_solve(): full_moduli = lax.all_gather(moduli_slab, 'vox', axis=1, tiled=True)  17.9 us
    all_to_all x1, waiting for transfers between devices, micro_solve(): lax.all_to_all(updated.reshape(7, per_rank, ranks_vox, thickness, VOX_PLA...  14.3 us
    all_to_all x1, starting transfers between devices, local(): lax.all_to_all(jnp.stack(jnp.split(strain_rows, lax.axis_size('macro'), a...  13.8 us
    unnamed x31, local copies, waits for them, and re-layouts  9.7 us
    dot_general x4, matrix products, spectral_correction(): jnp.dot(back_imag, sin_plane, precision=FULL_PREC)  9.12 us
    dot_general x4, matrix products, spectral_correction(): imag_plane = -jnp.dot(stress, sin_plane, precision=FULL_PREC)  8.94 us
  transfers between devices with their start and end apart: 8, of which 5 were waited for; matrix products, arithmetic and copies ran while one was open for 17% of the time, Pallas kernels for 0%

profile of v1, /device:TPU:0, one launch (start us, length us, event | category | flops | bytes accessed | tf_op | source)
XLA Modules:
  0.0 259.7 jit_solution(12803455570756755903)
XLA Ops:
  6.4 7.2 %all-to-all-start.1 = ((f32[1,16,3]{2,0,1:T(1,128)}), f32[1,16,3]{2,0,1:T(1,128)S(1)}, u32[]{:S(2)}, u32[]{:S(2)}) async-start(f32[1,16,3]{2,0,1:T(1,128)} %bitcast.30), calls=%async_computation.1 | async-start | bytes 16384 | tf_op jit(solution)/shard_map/all_to_all | solution.py:252
  15.0 2.8 %gather_fusion.4 = f32[48,7,8,256]{3,2,1,0:T(8,128)S(1)} fusion(f32[7,64,8,256]{3,2,1,0:T(8,128)} %param.20, s32[1024]{0:T(1024)S(1)} %get-tuple-element.240), kind=kCustom, calls=%fused_computation.4 | custom fusion | bytes 5505216 | tf_op jit(solution)/shard_map/gather | solution.py:242
  17.8 1.8 multiply_bitcast_fusion
  20.3 4.2 %compare_select_fusion.3 = (f32[256,1]{0,1:T(1,128)S(1)}, f32[256,1]{0,1:T(1,128)S(1)}) fusion(f32[]{:T(128)} %bitcast.70, f32[]{:T(128)} %bitcast.71, f32[]{:T(128)} %bitcast.72, f32[]{:T(128)} %bitcast.73, f32[]{:T(128)} %bitcast.74, f32[]{:T(128)} %bitcast.76, f32[]{:T(128)} %bitcast.75), kind=kLoop, calls=%fused_computation.522 | loop fusion | flops 10752 | bytes 2076 | tf_op jit(solution)/shard_map/gather | solution.py:143
  24.5 5.5 %broadcast_multiply_fusion = (f32[256]{0:T(256)S(1)}, f32[256]{0:T(256)S(1)}) fusion(pred[256]{0:T(512)(128)(4,1)S(1)} %compare_reduce_fusion.1, pred[256]{0:T(512)(128)(4,1)S(1)} %compare_reduce_fusion.2, pred[256]{0:T(512)(128)(4,1)S(1)} %compare_reduce_fusion.3, pred[256]{0:T(512)(128)(4,1)S(1)} %compare_reduce_fusion.4, ...), kind=kLoop, calls=%fused_computation.591 | loop fusion | flops 2560 | bytes 5412 | tf_op jit(solution)/shard_map/mul | solution.py:114
  30.0 5.5 %broadcast_multiply_fusion.1 = (f32[256]{0:T(256)S(1)}, f32[256]{0:T(256)S(1)}) fusion(pred[256]{0:T(512)(128)(4,1)S(1)} %compare_reduce_fusion.10, pred[256]{0:T(512)(128)(4,1)S(1)} %compare_reduce_fusion.11, pred[256]{0:T(512)(128)(4,1)S(1)} %compare_reduce_fusion.12, pred[256]{0:T(512)(128)(4,1)S(1)} %compare_reduce_fusion.13, ...), kind=kLoop, calls=%fused_computation.592 | loop fusion | flops 2560 | bytes 5412 | tf_op jit(solution)/shard_map/mul | solution.py:113
  35.6 6.0 %all-to-all-start.2 = ((f32[7,48,8,256]{3,2,0,1:T(8,128)}), f32[7,48,8,256]{3,2,0,1:T(8,128)S(1)}, u32[]{:S(2)}, u32[]{:S(2)}) async-start(f32[7,48,8,256]{3,2,0,1:T(8,128)} %multiply_bitcast_fusion), calls=%async_computation.2 | async-start | bytes 5505024 | tf_op jit(solution)/shard_map/all_to_all | solution.py:245
  53.7 40.3 %all-to-all-done.2 = f32[7,48,8,256]{3,2,0,1:T(8,128)S(1)} async-done(((f32[7,48,8,256]{3,2,0,1:T(8,128)}), f32[7,48,8,256]{3,2,0,1:T(8,128)S(1)}, u32[]{:S(2)}, u32[]{:S(2)}) %all-to-all-start.2) | async-done | bytes 2752544 | tf_op jit(solution)/shard_map/all_to_all | solution.py:245
  94.0 13.8 %all-to-all-start = ((f32[16,6,3]{1,2,0:T(4,128)}), f32[16,6,3]{1,2,0:T(4,128)S(1)}, u32[]{:S(2)}, u32[]{:S(2)}) async-start(f32[16,6,3]{1,2,0:T(4,128)} %constant_dynamic-update-slice_fusion), calls=%async_computation | async-start | bytes 65536 | tf_op jit(solution)/shard_map/all_to_all | solution.py:247
  107.9 1.8 copy.340
  109.7 2.4 gather_fusion.5
  112.1 1.2 copy.342
  114.5 3.6 %all-to-all-start.3 = ((f32[7,2,12,8,256]{4,3,2,0,1:T(8,128)}), f32[7,2,12,8,256]{4,3,2,0,1:T(8,128)S(1)}, u32[]{:S(2)}, u32[]{:S(2)}) async-start(f32[7,2,12,8,256]{4,3,2,0,1:T(8,128)} %copy.342), calls=%async_computation.3 | async-start | bytes 2752512 | tf_op jit(solution)/shard_map/all_to_all | solution.py:174
  118.2 17.9 %all_gather.6 = f32[4,16,256]{2,1,0:T(8,128)S(1)} all-gather(f32[4,8,256]{2,1,0:T(8,128)S(1)} %copy-done.1), channel_id=1, replica_groups=mesh['macro'=16,'vox'=2] {'vox'}, dimensions={1}, use_global_device_ids=true | all-gather | bytes 98304 | tf_op jit(solution)/shard_map/all_gather | solution.py:173
  138.2 2.1 fusion.42
  140.3 2.1 convolution_negate_fusion.3
  144.8 1.2 fusion.23
  146.0 1.2 fusion.22
  148.3 1.4 fusion.183
  152.1 1.2 fusion.21
  153.2 2.1 fusion.40
  155.4 2.2 fusion.7
  158.3 2.1 fusion.38
  160.4 2.5 convolution_negate_fusion.2
  165.3 1.2 fusion.19
  166.5 1.2 fusion.18
  171.2 1.2 fusion.16
  173.5 2.3 fusion.36
  175.8 2.2 fusion.5
  178.7 2.1 fusion.34
  180.9 2.1 convolution_negate_fusion.1
  185.4 1.4 fusion.15
  189.1 1.2 fusion.167
  193.8 2.1 fusion.32
  196.0 2.6 fusion.3
  199.3 2.1 fusion.30
  201.4 2.1 convolution_negate_fusion
  209.4 1.4 fusion.159
  214.3 2.1 fusion.28
  216.5 2.2 fusion.1
  219.8 4.4 %all-gather = f32[2,12,6]{1,2,0:T(8,128)S(1)} all-gather(f32[1,12,6]{1,2,0:T(8,128)S(1)} %multiply_bitcast_fusion.3), channel_id=1, replica_groups=mesh['macro'=16,'vox'=2] {'vox'}, dimensions={0}, use_global_device_ids=true | all-gather | bytes 864 | tf_op jit(solution)/shard_map/all_gather | solution.py:188
  225.3 5.4 %all-to-all-start.4 = ((f32[6,16,3]{0,2,1:T(4,128)}), f32[6,16,3]{0,2,1:T(4,128)S(1)}, u32[]{:S(2)}, u32[]{:S(2)}) async-start(f32[6,16,3]{0,2,1:T(4,128)} %copy.351), calls=%async_computation.4 | async-start | bytes 65536 | tf_op jit(solution)/shard_map/all_to_all | solution.py:259
  230.8 1.2 copy.371
  232.1 5.3 %all-to-all-done.4 = f32[6,16,3]{0,2,1:T(4,128)S(1)} async-done(((f32[6,16,3]{0,2,1:T(4,128)}), f32[6,16,3]{0,2,1:T(4,128)S(1)}, u32[]{:S(2)}, u32[]{:S(2)}) %all-to-all-start.4) | async-done | bytes 1184 | tf_op jit(solution)/shard_map/all_to_all | solution.py:259
  237.4 3.6 %all-to-all-start.5 = ((f32[7,12,2,8,256]{4,3,1,0,2:T(8,128)}), f32[7,12,2,8,256]{4,3,1,0,2:T(8,128)S(1)}, u32[]{:S(2)}, u32[]{:S(2)}) async-start(f32[7,12,2,8,256]{4,3,1,0,2:T(8,128)} %copy.371), calls=%async_computation.5 | async-start | bytes 2752512 | tf_op jit(solution)/shard_map/all_to_all | solution.py:189
  241.9 1.3 collective-permute-done.1
  243.9 14.3 %all-to-all-done.5 = f32[7,12,2,8,256]{4,3,1,0,2:T(8,128)S(1)} async-done(((f32[7,12,2,8,256]{4,3,1,0,2:T(8,128)}), f32[7,12,2,8,256]{4,3,1,0,2:T(8,128)S(1)}, u32[]{:S(2)}, u32[]{:S(2)}) %all-to-all-start.5) | async-done | bytes 1376288 | tf_op jit(solution)/shard_map/all_to_all | solution.py:189
  258.3 1.2 copy.361
  (202 shorter events, 58.9 us)
Async XLA Ops:
  5.0 36.7 %collective-permute-start = (f32[3,16]{0,1:T(8,128)S(1)}, f32[3,16]{0,1:T(8,128)S(1)}, u32[]{:S(2)}, u32[]{:S(2)}) collective-permute-start(f32[3,16]{0,1:T(8,128)S(1)} %bitcast.649), channel_id=1, source_target_pairs={{30,0},{0,2},{2,4},{4,6},{6,8},{8,10},{10,12},{12,14},{14,16},{16,... | collective-permute-start | bytes 584 | tf_op jit(solution)/shard_map/ppermute | solution.py:20
  6.4 29.2 %all-to-all-start.1 = ((f32[1,16,3]{2,0,1:T(1,128)}), f32[1,16,3]{2,0,1:T(1,128)S(1)}, u32[]{:S(2)}, u32[]{:S(2)}) async-start(f32[1,16,3]{2,0,1:T(1,128)} %bitcast.30), calls=%async_computation.1 | async-start | bytes 16384 | tf_op jit(solution)/shard_map/all_to_all | solution.py:252
  35.6 7.3 %copy-start = (f32[3,8,64]{2,1,0:T(8,128)S(1)}, f32[3,8,64]{2,1,0:T(8,128)}, u32[]{:S(2)}) copy-start(f32[3,8,64]{2,1,0:T(8,128)} %param.15) | copy-start | bytes 18436
  35.6 7.4 %copy-start.3 = (f32[2,64]{1,0:T(2,128)S(1)}, f32[2,64]{1,0:T(2,128)}, u32[]{:S(2)}) copy-start(f32[2,64]{1,0:T(2,128)} %param.17) | copy-start | bytes 1540
  35.6 58.4 %all-to-all-start.2 = ((f32[7,48,8,256]{3,2,0,1:T(8,128)}), f32[7,48,8,256]{3,2,0,1:T(8,128)S(1)}, u32[]{:S(2)}, u32[]{:S(2)}) async-start(f32[7,48,8,256]{3,2,0,1:T(8,128)} %multiply_bitcast_fusion), calls=%async_computation.2 | async-start | bytes 5505024 | tf_op jit(solution)/shard_map/all_to_all | solution.py:245
  94.0 20.5 %all-to-all-start = ((f32[16,6,3]{1,2,0:T(4,128)}), f32[16,6,3]{1,2,0:T(4,128)S(1)}, u32[]{:S(2)}, u32[]{:S(2)}) async-start(f32[16,6,3]{1,2,0:T(4,128)} %constant_dynamic-update-slice_fusion), calls=%async_computation | async-start | bytes 65536 | tf_op jit(solution)/shard_map/all_to_all | solution.py:247
  113.4 4.8 %copy-start.1 = (f32[4,8,256]{2,1,0:T(8,128)S(1)}, f32[4,8,256]{2,1,0:T(8,128)}, u32[]{:S(2)}) copy-start(f32[4,8,256]{2,1,0:T(8,128)} %param.21) | copy-start | bytes 98308
  114.5 22.6 %all-to-all-start.3 = ((f32[7,2,12,8,256]{4,3,2,0,1:T(8,128)}), f32[7,2,12,8,256]{4,3,2,0,1:T(8,128)S(1)}, u32[]{:S(2)}, u32[]{:S(2)}) async-start(f32[7,2,12,8,256]{4,3,2,0,1:T(8,128)} %copy.342), calls=%async_computation.3 | async-start | bytes 2752512 | tf_op jit(solution)/shard_map/all_to_all | solution.py:174
  225.3 12.1 %all-to-all-start.4 = ((f32[6,16,3]{0,2,1:T(4,128)}), f32[6,16,3]{0,2,1:T(4,128)S(1)}, u32[]{:S(2)}, u32[]{:S(2)}) async-start(f32[6,16,3]{0,2,1:T(4,128)} %copy.351), calls=%async_computation.4 | async-start | bytes 65536 | tf_op jit(solution)/shard_map/all_to_all | solution.py:259
  232.1 9.2 %copy-start.4 = (f32[64]{0:T(128)S(1)}, f32[64]{0:T(128)}, u32[]{:S(2)}) copy-start(f32[64]{0:T(128)} %param.16) | copy-start | bytes 772
  232.1 9.3 %copy-start.2 = (s32[8,64]{1,0:T(8,128)S(1)}, s32[8,64]{1,0:T(8,128)}, u32[]{:S(2)}) copy-start(s32[8,64]{1,0:T(8,128)} %param.13) | copy-start | bytes 6148
  232.1 11.1 %copy-start.5 = (f32[3,64]{1,0:T(4,128)S(1)}, f32[3,64]{1,0:T(4,128)}, u32[]{:S(2)}) copy-start(f32[3,64]{1,0:T(4,128)} %param.12) | copy-start | bytes 2308
  232.1 11.1 %copy-start.6 = (s32[16]{0:T(128)S(1)}, s32[16]{0:T(128)}, u32[]{:S(2)}) copy-start(s32[16]{0:T(128)} %param.14) | copy-start | bytes 196
  237.4 20.9 %all-to-all-start.5 = ((f32[7,12,2,8,256]{4,3,1,0,2:T(8,128)}), f32[7,12,2,8,256]{4,3,1,0,2:T(8,128)S(1)}, u32[]{:S(2)}, u32[]{:S(2)}) async-start(f32[7,12,2,8,256]{4,3,1,0,2:T(8,128)} %copy.371), calls=%async_computation.5 | async-start | bytes 2752512 | tf_op jit(solution)/shard_map/all_to_all | solution.py:189
  241.7 1.5 collective-permute-start.1
